TPU v7x, 256 devices: a whole 4x4x8 slice. The times are simulated.
256 devices in a mesh: expert: 128 (over x, z, y), half: 2 (over core).
Axes of the slice: x: 4, y: 4, z: 8, core: 2. Of those that a mesh axis runs over, the one named last changes fastest.
Arguments:
- tokens: bfloat16 [8192, 2048], P('expert'), may hold values from -6 to 6
- routes: int32 [8192, 8], P('expert'), may hold values from 0 to 127, all different within a row; in each aligned block of 64 rows (0 to 63, 64 to 127, ...) at most 8 rows name the same one
- gates: float32 [8192, 8], P('expert'), may hold values from 0.05 to 0.5
- cotangent: bfloat16 [8192, 2048], P('expert'), may hold values from -1.5 to 1.5
- w_gate: bfloat16 [128, 2048, 768], P('expert', None, 'half'), may hold values from -0.125 to 0.125
- w_up: bfloat16 [128, 2048, 768], P('expert', None, 'half'), may hold values from -0.125 to 0.125
- w_down: bfloat16 [128, 768, 2048], P('expert', 'half'), may hold values from -0.21875 to 0.21875
Outputs:
- mixed: bfloat16 [8192, 2048], P('expert')
- token_grad: bfloat16 [8192, 2048], P('expert')
- gate_grad: float32 [8192, 8], P('expert')
- grad_gate: bfloat16 [128, 2048, 768], P('expert', None, 'half')
- grad_up: bfloat16 [128, 2048, 768], P('expert', None, 'half')
- grad_down: bfloat16 [128, 768, 2048], P('expert', 'half')
Inputs may be any that keep to these rules, and one draw needn't show every extreme that they name: `routes`: each token names 8 different experts. Among the 64 tokens of one index of the expert axis, no expert is named more than 8 times, a bound that some block reaches.
All inputs are finite; a program needn't handle non-finite values.
Results may differ from a plain program's by a relative error of at most 0.0064.
Values may be sent and summed in bfloat16 or wider, within the bound.
A program may use at most 128 MiB of HBM per device.

v0:
```python
import jax
import jax.numpy as jnp
from jax import lax
from jax.sharding import PartitionSpec as P


def side_by_side(arrays, axis, split_dim, concat_dim, along):
    both = jnp.concatenate(arrays, axis=along)
    filled, at, finished = (
        lax.all_to_all(both, axis, split_axis=split_dim, concat_axis=concat_dim, tiled=True),
        0,
        [],
    )
    for a in arrays:
        finished.append(lax.slice_in_dim(filled, at, at + a.shape[along], axis=along))
        at += a.shape[along]
    return tuple(finished)


def sent_together(arrays, axis, dim, along):
    ends, at = ([], 0)
    for a in arrays[:-1]:
        at += a.shape[along]
        ends.append(at)
    both = jnp.concatenate(arrays, axis=along)
    return tuple(jnp.split(lax.all_gather(both, axis, axis=dim, tiled=True), ends, axis=along))


def sent_together_2(arrays, axis, dim, along):
    ends, at = ([], 0)
    for a in arrays[:-1]:
        at += a.shape[along]
        ends.append(at)
    both = jnp.concatenate(arrays, axis=along)
    return tuple(
        jnp.split(lax.psum_scatter(both, axis, scatter_dimension=dim, tiled=True), ends, axis=along)
    )


def contract(left, right, left_dim, right_dim):
    return lax.dot_general(
        left, right, (((left_dim,), (right_dim,)), ((), ())), preferred_element_type=jnp.float32
    )


def body(tokens, routes, gates, cotangent, w_gate, w_up, w_down):
    token_count, features = tokens.shape
    top_k = routes.shape[1]
    senders = lax.axis_size("expert")
    halves = lax.axis_size("half")
    experts = w_gate.shape[0] * senders
    slot_count = token_count * top_k
    capacity = 2 * slot_count // experts
    routed = routes.reshape(slot_count)
    onehot = (routed[:, None] == jnp.arange(experts, dtype=jnp.int32)[None, :]).astype(jnp.int32)
    placed = jnp.sum((jnp.cumsum(onehot, axis=0) - onehot) * onehot, axis=1)
    target = routed * capacity + placed
    slot_table = jnp.full((experts * capacity,), slot_count, jnp.int32)
    slot_table = slot_table.at[target].set(jnp.arange(slot_count, dtype=jnp.int32))
    present = slot_table < slot_count
    clipped = jnp.minimum(slot_table, slot_count - 1)
    owners = clipped // top_k
    picked = tokens[owners]
    rows_send = jnp.where(present[:, None], picked, jnp.zeros_like(picked)).reshape(
        experts, capacity, features
    )
    weighted = gates.reshape(slot_count)[clipped][:, None] * cotangent[owners].astype(jnp.float32)
    scaled_send = (
        jnp.where(present[:, None], weighted, 0.0)
        .astype(jnp.bfloat16)
        .reshape(experts, capacity, features)
    )
    half_width = features // halves
    offset = lax.axis_index("half") * half_width
    rows_part = lax.dynamic_slice_in_dim(rows_send, offset, half_width, 2)
    scaled_part = lax.dynamic_slice_in_dim(scaled_send, offset, half_width, 2)
    rows_moved, scaled_moved = side_by_side((rows_part, scaled_part), "expert", 0, 0, 1)
    rows_in, scaled_in = sent_together((rows_moved, scaled_moved), "half", 2, 0)
    received = senders * capacity
    rows_in = rows_in.reshape(received, features)
    scaled_in = scaled_in.reshape(received, features)
    wgate = w_gate[0]
    wupper = w_up[0]
    wdown = w_down[0]
    pre_gate = jnp.dot(rows_in, wgate, preferred_element_type=jnp.float32)
    pre_up = jnp.dot(rows_in, wupper, preferred_element_type=jnp.float32)
    sigma = jax.nn.sigmoid(pre_gate)
    hidden = (pre_gate * sigma * pre_up).astype(jnp.bfloat16)
    out_part = jnp.dot(hidden, wdown, preferred_element_type=jnp.float32)
    back_hidden = contract(scaled_in, wdown, 1, 1)
    d_up = (back_hidden * pre_gate * sigma).astype(jnp.bfloat16)
    d_gate = (back_hidden * pre_up * sigma * (1.0 + pre_gate * (1.0 - sigma))).astype(jnp.bfloat16)
    grad_part = contract(d_gate, wgate, 1, 1) + contract(d_up, wupper, 1, 1)
    grad_gate = contract(rows_in, d_gate, 0, 0).astype(jnp.bfloat16)[None]
    grad_up = contract(rows_in, d_up, 0, 0).astype(jnp.bfloat16)[None]
    grad_down = contract(hidden, scaled_in, 0, 0).astype(jnp.bfloat16)[None]
    out_mine, grad_mine = sent_together_2((out_part, grad_part), "half", 1, 0)
    out_mine = out_mine.astype(jnp.bfloat16)
    grad_mine = grad_mine.astype(jnp.bfloat16)
    out_block = out_mine.reshape(senders, capacity, features // halves)
    grad_block = grad_mine.reshape(senders, capacity, features // halves)
    out_back, grad_back = side_by_side((out_block, grad_block), "expert", 0, 0, 1)
    out_home, grad_home = sent_together((out_back, grad_back), "half", 2, 0)
    out_slots = out_home.reshape(experts * capacity, features)[target].reshape(
        token_count, top_k, features
    )
    grad_slots = grad_home.reshape(experts * capacity, features)[target].reshape(
        token_count, top_k, features
    )
    out_float = out_slots.astype(jnp.float32)
    mixed = jnp.sum(gates[:, :, None] * out_float, axis=1).astype(jnp.bfloat16)
    gate_grad = jnp.sum(cotangent.astype(jnp.float32)[:, None, :] * out_float, axis=2)
    token_grad = jnp.sum(grad_slots.astype(jnp.float32), axis=1).astype(jnp.bfloat16)
    return (mixed, token_grad, gate_grad, grad_gate, grad_up, grad_down)


def solution(mesh):
    placed = (
        P("expert", None),
        P("expert", None),
        P("expert", None),
        P("expert", None),
        P("expert", None, "half"),
        P("expert", None, "half"),
        P("expert", "half", None),
    )
    return jax.shard_map(
        body,
        mesh=mesh,
        in_specs=placed,
        out_specs=(
            P("expert", None),
            P("expert", None),
            P("expert", None),
            P("expert", None, "half"),
            P("expert", None, "half"),
            P("expert", "half", None),
        ),
        check_vma=False,
    )
```

profile of v0, /device:TPU:1, one launch (start us, length us, event | category | flops | bytes accessed | tf_op | source)
XLA Modules:
  0.0 407.5 jit_solution(14547028168022796952)
XLA Ops:
  7.2 0.8 broadcast_multiply_fusion
  8.1 0.8 copy.23
  8.8 0.1 eq.29
  9.1 0.1 mul.80
  9.2 0.1 copy.25
  9.3 0.2 fusion.22
  9.6 0.2 fusion.21
  9.9 2.4 scatter_custom_fusion
  12.4 0.8 copy.21
  13.2 0.1 broadcast_in_dim.48
  13.3 6.9 %gather_fusion.1 = f32[1024]{0:T(1024)S(1)} fusion(f32[512]{0:T(512)S(1)} %reshape.120, s32[1024]{0:T(1024)S(1)} %get-tuple-element.26), kind=kCustom, calls=%fused_computation.1 | custom fusion | bytes 12288 | tf_op jit(solution)/shard_map/gather | solution.py:67
  20.3 6.0 %gather_fusion.2 = bf16[1024,2048]{1,0:T(8,128)(2,1)} fusion(bf16[64,2048]{1,0:T(8,128)(2,1)S(1)} %copy-done.2, s32[1024]{0:T(1024)S(1)} %get-tuple-element.25), kind=kCustom, calls=%fused_computation.2 | custom fusion | bytes 8392704 | tf_op jit(solution)/shard_map/gather | solution.py:67
  26.3 6.1 %gather_fusion = bf16[1024,2048]{1,0:T(8,128)(2,1)} fusion(bf16[64,2048]{1,0:T(8,128)(2,1)S(1)} %copy-done.3, s32[1024]{0:T(1024)S(1)} %get-tuple-element.25), kind=kCustom, calls=%fused_computation | custom fusion | bytes 8392704 | tf_op jit(solution)/shard_map/gather | solution.py:63
  32.4 2.2 dynamic-slice_select_fusion
  34.6 0.6 copy-done.4
  35.2 0.6 fusion.3
  35.8 0.6 pad_maximum_fusion.1
  36.5 109.3 %all_to_all.10 = bf16[128,16,1024]{2,1,0:T(8,128)(2,1)S(1)} all-to-all(bf16[128,16,1024]{2,1,0:T(8,128)(2,1)S(1)} %pad_maximum_fusion.1), channel_id=1, replica_groups=mesh['expert'=128,'half'=2] {'expert'}, dimensions={0} | all-to-all | bytes 8388608 | tf_op jit(solution)/shard_map/all_to_all | solution.py:10
  145.8 0.5 fusion.32
  146.2 2.3 pad_maximum_fusion.2
  148.6 0.2 reduce-scatter.2.cloned.1.call-start
  148.8 24.7 %all-gather.3.cloned.1.call-done = bf16[256,8,2048]{2,1,0:T(8,128)(2,1)} async-done(((bf16[256,8,1024]{2,1,0:T(8,128)(2,1)}), bf16[256,8,2048]{2,1,0:T(8,128)(2,1)}) %all-gather.3.cloned.1.call-update) | async-done | bytes 8388624 | tf_op jit(solution)/shard_map/all_gather | solution.py:26
  173.5 5.2 %fusion.5 = f32[1024,384]{1,0:T(8,128)S(1)} fusion(bf16[256,8,2048]{2,1,0:T(8,128)(2,1)} %all-gather.3.cloned.1.call-done, bf16[1,384,2048]{2,1,0:T(8,128)(2,1)} %param.13), kind=kOutput, calls=%fused_computation.24 | convolution fusion | flops 1610612736 | bytes 7340032 | tf_op jit(solution)/shard_map/dot_general | solution.py:41
  178.7 2.3 fusion.8
  181.0 2.9 multiply_convert_fusion.2
  184.0 2.4 fusion.17
  186.4 2.3 fusion.13
  188.8 2.4 convolution_add_fusion
  191.2 6.2 %pad_maximum_fusion = f32[2048,2048]{1,0:T(8,128)} fusion(f32[1024,2048]{1,0:T(8,128)S(1)} %convolution_add_fusion, f32[1024,2048]{1,0:T(8,128)S(1)} %fusion.13), kind=kLoop, calls=%fused_computation.6 | loop fusion | flops 4194304 | bytes 33554432 | tf_op jit(solution)/shard_map/concatenate | solution.py:34
  197.4 0.3 all-gather.5.cloned.1.call-start
  197.6 32.6 %reduce-scatter.2.cloned.1.call-done = f32[2048,1024]{1,0:T(8,128)} async-done(((f32[2048,2048]{1,0:T(8,128)}), f32[2048,1024]{1,0:T(8,128)}) %reduce-scatter.2.cloned.1.call-update) | async-done | bytes 8388624 | tf_op jit(solution)/shard_map/reduce_scatter | solution.py:36
  230.3 4.0 convert.7
  234.3 0.4 slice_bitcast_fusion.19
  234.8 0.6 pad_maximum_fusion.3
  235.4 107.0 %all_to_all.11 = bf16[128,16,1024]{2,1,0:T(8,128)(2,1)S(1)} all-to-all(bf16[128,16,1024]{2,1,0:T(8,128)(2,1)S(1)} %pad_maximum_fusion.3), channel_id=1, replica_groups=mesh['expert'=128,'half'=2] {'expert'}, dimensions={0} | all-to-all | bytes 8388608 | tf_op jit(solution)/shard_map/all_to_all | solution.py:10
  342.4 0.5 fusion.31
  342.9 2.3 pad_maximum_fusion.4
  345.3 1.0 copy-done.12
  346.3 5.3 %fusion.11 = bf16[1,384,2048]{2,1,0:T(8,128)(2,1)} fusion(bf16[1024,384]{1,0:T(8,128)(2,1)S(1)} %copy-done.12, bf16[256,8,2048]{2,1,0:T(8,128)(2,1)} %all-gather.3.cloned.1.call-done), kind=kOutput, calls=%fused_computation.32 | convolution fusion | flops 1611399168 | bytes 6553600 | tf_op jit(solution)/shard_map/dot_general | solution.py:41
  351.6 5.9 %fusion.9 = bf16[1,2048,384]{2,1,0:T(8,128)(2,1)} fusion(bf16[1024,384]{1,0:T(8,128)(2,1)S(1)} %copy-done.8, bf16[256,8,2048]{2,1,0:T(8,128)(2,1)} %all-gather.3.cloned.1.call-done), kind=kOutput, calls=%fused_computation.30 | convolution fusion | flops 1611399168 | bytes 6553600 | tf_op jit(solution)/shard_map/dot_general | solution.py:41
  357.5 3.6 fusion.10
  361.1 8.7 %all-gather.5.cloned.1.call-done = bf16[256,8,2048]{2,1,0:T(8,128)(2,1)} async-done(((bf16[256,8,1024]{2,1,0:T(8,128)(2,1)}), bf16[256,8,2048]{2,1,0:T(8,128)(2,1)}) %all-gather.5.cloned.1.call-update) | async-done | bytes 8388624 | tf_op jit(solution)/shard_map/all_gather | solution.py:26
  369.8 6.0 %slice_bitcast_fusion = (bf16[1024,2048]{1,0:T(8,128)(2,1)}, bf16[1024,2048]{1,0:T(8,128)(2,1)}) fusion(bf16[256,8,2048]{2,1,0:T(8,128)(2,1)} %all-gather.5.cloned.1.call-done), kind=kLoop, calls=%fused_computation.12 | loop fusion | bytes 16777216 | tf_op jit(solution)/shard_map/reshape | solution.py:107
  375.8 8.0 %gather_fusion.4 = bf16[512,2048]{1,0:T(8,128)(2,1)} fusion(bf16[1024,2048]{1,0:T(8,128)(2,1)} %get-tuple-element.14, s32[1024]{0:T(1024)S(1)} %pad_clamp_fusion), kind=kCustom, calls=%fused_computation.4 | custom fusion | bytes 4196352 | tf_op jit(solution)/shard_map/gather | solution.py:107
  383.8 8.4 %gather_fusion.3 = bf16[512,2048]{1,0:T(8,128)(2,1)} fusion(bf16[1024,2048]{1,0:T(8,128)(2,1)} %get-tuple-element.15, s32[1024]{0:T(1024)S(1)} %pad_clamp_fusion), kind=kCustom, calls=%fused_computation.3 | custom fusion | bytes 4196352 | tf_op jit(solution)/shard_map/gather | solution.py:104
  392.2 3.7 bitcast_reduce_fusion
  395.9 4.0 fusion.1
  399.9 0.7 copy.28
  (51 shorter events, 0.7 us)
Async XLA Ops:
  7.2 173.9 %copy-start = (bf16[1,2048,384]{2,1,0:T(8,128)(2,1)S(1)}, bf16[1,2048,384]{2,1,0:T(8,128)(2,1)}, u32[]{:S(2)}) copy-start(bf16[1,2048,384]{2,1,0:T(8,128)(2,1)} %param.12) | copy-start | bytes 4718596
  7.2 13.1 %copy-start.2 = (bf16[64,2048]{1,0:T(8,128)(2,1)S(1)}, bf16[64,2048]{1,0:T(8,128)(2,1)}, u32[]{:S(2)}) copy-start(bf16[64,2048]{1,0:T(8,128)(2,1)} %param.10) | copy-start | bytes 786436
  7.2 166.3 %all-gather.3.cloned.1.call-start = ((), (), s32[]{:S(2)}) async-start(), calls=%async_computation.3 | async-start | bytes 12582912 | tf_op jit(solution)/shard_map/all_gather | solution.py:26
  20.3 6.0 %copy-start.3 = (bf16[64,2048]{1,0:T(8,128)(2,1)S(1)}, bf16[64,2048]{1,0:T(8,128)(2,1)}, u32[]{:S(2)}) copy-start(bf16[64,2048]{1,0:T(8,128)(2,1)} %param.7) | copy-start | bytes 786436
  32.4 2.8 copy-start.4
  148.6 30.1 %copy-start.5 = (bf16[1,2048,384]{2,1,0:T(8,128)(2,1)S(1)}, bf16[1,2048,384]{2,1,0:T(8,128)(2,1)}, u32[]{:S(2)}) copy-start(bf16[1,2048,384]{2,1,0:T(8,128)(2,1)} %param.11) | copy-start | bytes 4718596
  148.6 81.7 %reduce-scatter.2.cloned.1.call-start = ((), (), s32[]{:S(2)}) async-start(), calls=%async_computation.4 | async-start | bytes 25165824 | tf_op jit(solution)/shard_map/reduce_scatter | solution.py:36
  173.5 5.2 %copy-start.13 = (bf16[256,8,2048]{2,1,0:T(8,128)(2,1)S(1)}, bf16[256,8,2048]{2,1,0:T(8,128)(2,1)}, u32[]{:S(2)}) copy-start(bf16[256,8,2048]{2,1,0:T(8,128)(2,1)} %all-gather.3.cloned.1.call-done) | copy-start | bytes 25165828
  183.9 2.4 copy-start.7
  184.0 2.4 copy-start.11
  184.0 4.8 %copy-start.9 = (bf16[1024,384]{1,0:T(8,128)(2,1)}, bf16[1024,384]{1,0:T(8,128)(2,1)S(1)}, u32[]{:S(2)}) copy-start(bf16[1024,384]{1,0:T(8,128)(2,1)S(1)} %get-tuple-element.24) | copy-start | bytes 2359300
  184.0 2.4 copy-start.6
  197.4 172.4 %all-gather.5.cloned.1.call-start = ((), (), s32[]{:S(2)}) async-start(), calls=%async_computation.5 | async-start | bytes 12582912 | tf_op jit(solution)/shard_map/all_gather | solution.py:26
  345.2 1.1 copy-start.12
  346.3 5.3 %copy-start.8 = (bf16[1024,384]{1,0:T(8,128)(2,1)S(1)}, bf16[1024,384]{1,0:T(8,128)(2,1)}, u32[]{:S(2)}) copy-start(bf16[1024,384]{1,0:T(8,128)(2,1)} %copy-done.7) | copy-start | bytes 2359300
  346.3 11.2 %slice-start = ((s8[8388608]{0:T(1024)(128)(4,1)}), s8[4194304]{0:T(1024)(128)(4,1)S(1)}, s32[]{:S(2)}) async-start(s8[8388608]{0:T(1024)(128)(4,1)} %bitcast.90), calls=%async_computation.6 | async-start | bytes 8388608
  351.6 5.9 %copy-start.10 = (bf16[1024,384]{1,0:T(8,128)(2,1)S(1)}, bf16[1024,384]{1,0:T(8,128)(2,1)}, u32[]{:S(2)}) copy-start(bf16[1024,384]{1,0:T(8,128)(2,1)} %copy-done.9) | copy-start | bytes 2359300
  351.6 5.9 %slice-start.1 = ((s8[8388608]{0:T(1024)(128)(4,1)}), s8[4194304]{0:T(1024)(128)(4,1)S(1)}, s32[]{:S(2)}) async-start(s8[8388608]{0:T(1024)(128)(4,1)} %bitcast.90), calls=%async_computation.7 | async-start | bytes 8388608
  383.8 16.7 %copy-start.1 = (bf16[1,2048,384]{2,1,0:T(8,128)(2,1)S(1)}, bf16[1,2048,384]{2,1,0:T(8,128)(2,1)}, u32[]{:S(2)}) copy-start(bf16[1,2048,384]{2,1,0:T(8,128)(2,1)} %param.12) | copy-start | bytes 4718596
Sparse Core Ops, SparseCore 0:
  148.7 24.7 all-gather.2
  197.5 32.7 reduce-scatter.1
  345.3 24.4 all-gather.4
where the time goes:
time: 413 us; the launch traced here: 407 us
  blocking collectives  216 us (52%)
  waiting for transfers between devices  66.1 us (16%)
  local copies, waits for them, and re-layouts  49.8 us (12%)
  matrix products  32.3 us (8%)
  other arithmetic  28 us (7%)
  between operations  14.5 us (4%)
    all_to_all x2, blocking collectives, side_by_side(): lax.all_to_all(both, axis, split_axis=split_dim, concat_axis=concat_dim,...  216 us
    all_gather x2, waiting for transfers between devices, sent_together(): lax.all_gather(both, axis, axis=dim, tiled=True)  33.4 us
    reduce_scatter x1, waiting for transfers between devices, sent_together_2(): lax.psum_scatter(both, axis, scatter_dimension=dim, tiled=True)  32.6 us
    dot_general x6, matrix products, contract(): lax.dot_general(left, right, (((left_dim,), (right_dim,)), ((), ())), pre...  24.7 us
    gather x1, local copies, waits for them, and re-layouts, body(): out_home.reshape(experts * capacity, features)[target]  8.35 us
  transfers between devices with their start and end apart: 3, of which 3 were waited for; matrix products, arithmetic and copies ran while one was open for 4% of the time, Pallas kernels for 0%

commit v1 on v0

v1 whole, which is shorter than its diff:
```python
import jax
import jax.numpy as jnp
from jax import lax
from jax.experimental import pallas as pl
from jax.experimental.pallas import tpu as pltpu
from jax.sharding import PartitionSpec as P

MESH = pl.DeviceIdType.MESH
NX, NZ, NY = 4, 8, 4
PLANE = NX * NY
TOK = 64
D = 2048
HALF = D // 2
HID = 384
TOP = 8
CAP = 8
STEPS = 4
ROWS = PLANE * 2 * CAP
OFFSETS = ((-1, 1), (4, -3), (3, -2), (0, 2))
BF = jnp.bfloat16
F32 = jnp.float32


def dot(a, b, ca, cb):
    return lax.dot_general(a, b, (((ca,), (cb,)), ((), ())), preferred_element_type=F32)


def kernel(
    tok, cot, routes, gates, wg_h, wu_h, wd_h,
    mixed_o, tgrad_o, gg_o, gwg_o, gwu_o, gwd_o,
    gath, meta, mats, sel, rows, scal, wg, wu, wd, own, psend, precv, ret, rret,
    zs, zq, zrx, zqr, fin, finr, finq, finqr, hid, dgu, gwg, gwu, gwd,
    w_sem, zt_s, zt_r, pd_s, pd_r, cx_s, cx_r, px_s, px_r, pr_s, pr_r,
    zr_s, zr_r, zq_s, zq_r, f_s, f_r, o_sem,
):
    e = lax.axis_index("expert")
    h = lax.axis_index("half")
    x, z, y = e // (NZ * NY), (e // NY) % NZ, e % NY
    me = x * NY + y
    hs = pl.multiple_of(h * HALF, HALF)
    ho = pl.multiple_of((1 - h) * HALF, HALF)

    def at_z(dz):
        return ((x * NZ + (z + dz + NZ) % NZ) * NY + y, h)

    def in_plane(r):
        xx = (x + r // NY) % NX
        yy = (y + r % NY) % NY
        return ((xx * NZ + z) * NY + yy, h), xx * NY + yy

    partner = (e, 1 - h)

    loads = [
        pltpu.make_async_copy(src.at[0], dst, w_sem.at[i])
        for i, (src, dst) in enumerate(((wg_h, wg), (wu_h, wu), (wd_h, wd)))
    ]
    for c in loads:
        c.start()

    barrier = pltpu.get_barrier_semaphore()

    @pl.loop(1, PLANE)
    def _(r):
        pl.semaphore_signal(barrier, inc=1, device_id=in_plane(r)[0], device_id_type=MESH)

    @pl.loop(1, NZ)
    def _(r):
        pl.semaphore_signal(barrier, inc=1, device_id=at_z(r), device_id_type=MESH)

    pl.semaphore_signal(barrier, inc=1, device_id=partner, device_id_type=MESH)

    gath[z, 0:TOK, :] = tok[:, pl.ds(hs, HALF)]
    gath[z, TOK : 2 * TOK, :] = cot[:, pl.ds(hs, HALF)]
    meta[z] = jnp.zeros((TOK, 128), F32)
    meta[z, :, 0:TOP] = routes[...].astype(F32)
    meta[z, :, TOP : 2 * TOP] = gates[...]
    pl.semaphore_wait(barrier, PLANE - 1 + NZ - 1 + 1)

    def hop(stream, way, d, src_z):
        ref = meta.at[src_z] if stream == 2 else gath.at[src_z, pl.ds(stream * TOK, TOK)]
        return pltpu.make_async_remote_copy(
            src_ref=ref,
            dst_ref=ref,
            send_sem=zt_s.at[stream, way, d - 1],
            recv_sem=zt_r.at[stream, way, d - 1],
            device_id=at_z(1 if way == 0 else -1),
            device_id_type=MESH,
        )

    reach = ((4, 3), (3, 4), (4, 3))
    hops = []
    for way in (0, 1):
        for stream in (0, 1, 2):
            c = hop(stream, way, 1, z)
            c.start()
            hops.append(c)

    def arrive(d):
        for way in (0, 1):
            src = (z - d + NZ) % NZ if way == 0 else (z + d) % NZ
            for stream in (0, 1, 2):
                if d <= reach[stream][way]:
                    hop(stream, way, d, src).wait_recv()
                    if d + 1 <= reach[stream][way]:
                        c = hop(stream, way, d + 1, src)
                        c.start()
                        hops.append(c)

    lane = lax.broadcasted_iota(jnp.int32, (2 * TOK, ROWS), 1)
    row = lax.broadcasted_iota(jnp.int32, (2 * TOK, ROWS), 0)
    ids = ((lane // (NY * 2 * CAP)) * NZ + z) * NY + (lane // (2 * CAP)) % NY
    ids = jnp.where((lane // CAP) % 2 == row // TOK, ids, -1).astype(F32)
    place = (lane % CAP).astype(F32)

    def pair(s):
        a, b = OFFSETS[s]
        return (z + a + NZ) % NZ, (z + b + NZ) % NZ

    def both(ref, za, zb, lo, n):
        return jnp.concatenate([ref[za, lo : lo + n, :], ref[zb, lo : lo + n, :]], axis=0)

    def select(s):
        za, zb = pair(s)
        info = both(meta, za, zb, 0, TOK)
        named = jnp.zeros((2 * TOK, ROWS), F32)
        weight = jnp.zeros((2 * TOK, ROWS), F32)
        for k in range(TOP):
            hit = info[:, k : k + 1] == ids
            named = jnp.where(hit, 1.0, named)
            weight = jnp.where(hit, info[:, TOP + k : TOP + k + 1], weight)
        r0 = lax.broadcasted_iota(jnp.int32, (2 * TOK, 2 * TOK), 0)
        r1 = lax.broadcasted_iota(jnp.int32, (2 * TOK, 2 * TOK), 1)
        before = jnp.where(r1 < r0, 1.0, 0.0).astype(BF)
        placed = dot(before, named.astype(BF), 1, 0)
        one = jnp.where(placed == place, named, 0.0)
        weight = one * weight
        high = weight.astype(BF)
        low = (weight - high.astype(F32)).astype(BF)
        one = one.astype(BF)
        mats[s, 0 : 2 * TOK, :] = one
        mats[s, 2 * TOK : 4 * TOK, :] = high
        mats[s, 4 * TOK : 6 * TOK, :] = low
        tokens = both(gath, za, zb, 0, TOK)
        cots = both(gath, za, zb, TOK, TOK)
        sel[s, 0:ROWS, :] = dot(one, tokens, 0, 0).astype(BF)
        sel[s, ROWS : 2 * ROWS, :] = dot(
            jnp.concatenate([high, low], axis=0), jnp.concatenate([cots, cots], axis=0), 0, 0
        ).astype(BF)

    def block(p):
        return pl.ds(pl.multiple_of(p * 2 * CAP, 2 * CAP), 2 * CAP)

    def block_at(base, p):
        return pl.ds(pl.multiple_of(base + p * 2 * CAP, 2 * CAP), 2 * CAP)

    def dispatch(s):
        @pl.loop(1, PLANE)
        def _(r):
            dev, p = in_plane(r)
            for t, dst in ((0, rows), (1, scal)):
                pltpu.make_async_remote_copy(
                    src_ref=sel.at[s, block_at(t * ROWS, p)],
                    dst_ref=dst.at[block_at(s * ROWS, me), pl.ds(hs, HALF)],
                    send_sem=pd_s.at[s],
                    recv_sem=pd_r.at[s],
                    device_id=dev,
                    device_id_type=MESH,
                ).start()

        for t, dst in ((0, rows), (1, scal)):
            dst[block_at(s * ROWS, me), pl.ds(hs, HALF)] = sel[s, block_at(t * ROWS, me)]

    def bulk(sem):
        blocks = sel.at[0, pl.ds(0, 2 * ROWS - 4 * CAP)]
        return pltpu.make_async_copy(blocks, blocks, sem)

    arrive(1)
    select(0)
    dispatch(0)
    arrive(2)
    arrive(3)
    arrive(4)
    for s in range(1, STEPS):
        select(s)
        dispatch(s)

    for c in loads:
        c.wait()

    @pl.loop(0, STEPS)
    def _(s):
        at = pl.ds(pl.multiple_of(s * ROWS, ROWS), ROWS)
        bulk(pd_r.at[s]).wait()
        swaps = []
        for t, ref in ((0, rows), (1, scal)):
            c = pltpu.make_async_remote_copy(
                src_ref=ref.at[at, pl.ds(hs, HALF)],
                dst_ref=ref.at[at, pl.ds(hs, HALF)],
                send_sem=cx_s.at[s, t],
                recv_sem=cx_r.at[s, t],
                device_id=partner,
                device_id_type=MESH,
            )
            c.start()
            swaps.append(c)
        for c in swaps:
            c.wait()
        r = rows[at, :]
        pre_gate = dot(r, wg[...], 1, 0)
        pre_up = dot(r, wu[...], 1, 0)
        back = dot(scal[at, :], wd[...], 1, 1)
        sigma = jax.nn.sigmoid(pre_gate)
        hidden = (pre_gate * sigma * pre_up).astype(BF)
        d_up = (back * pre_gate * sigma).astype(BF)
        d_gate = (back * pre_up * sigma * (1.0 + pre_gate * (1.0 - sigma))).astype(BF)
        hid[at, :] = hidden
        dgu[at, 0:HID] = d_gate
        dgu[at, HID : 2 * HID] = d_up
        for base, dst in ((ho, None), (hs, own)):
            for q in range(2):
                f = pl.ds(pl.multiple_of(base + q * 512, 512), 512)
                g = dot(d_gate, wg[f, :], 1, 1) + dot(d_up, wu[f, :], 1, 1)
                o = dot(hidden, wd[:, f], 1, 0)
                if dst is None:
                    psend[s, 0:ROWS, q * 512 : (q + 1) * 512] = g.astype(BF)
                    psend[s, ROWS : 2 * ROWS, q * 512 : (q + 1) * 512] = o.astype(BF)
                else:
                    own[0:ROWS, q * 512 : (q + 1) * 512] = g
                    own[ROWS : 2 * ROWS, q * 512 : (q + 1) * 512] = o
            if dst is None:
                swap = pltpu.make_async_remote_copy(
                    src_ref=psend.at[s],
                    dst_ref=precv.at[s],
                    send_sem=px_s.at[s],
                    recv_sem=px_r.at[s],
                    device_id=partner,
                    device_id_type=MESH,
                )
                swap.start()
        swap.wait()
        ret[s] = (own[...] + precv[s].astype(F32)).astype(BF)

        @pl.loop(1, PLANE)
        def _(k):
            dev, p = in_plane(k)
            for t in (0, 1):
                pltpu.make_async_remote_copy(
                    src_ref=ret.at[s, block_at(t * ROWS, p)],
                    dst_ref=rret.at[s, block_at(t * ROWS, me)],
                    send_sem=pr_s.at[s],
                    recv_sem=pr_r.at[s],
                    device_id=dev,
                    device_id_type=MESH,
                ).start()

        for t in (0, 1):
            rret[s, block_at(t * ROWS, me), :] = ret[s, block_at(t * ROWS, me), :]

    @pl.loop(0, D // 256)
    def _(i):
        f = pl.ds(pl.multiple_of(i * 256, 256), 256)
        g = dot(rows[:, f], dgu[...], 0, 0)
        gwg[f, :] = g[:, 0:HID].astype(BF)
        gwu[f, :] = g[:, HID : 2 * HID].astype(BF)
        gwd[:, f] = dot(hid[...], scal[:, f], 0, 0).astype(BF)

    stores = [
        pltpu.make_async_copy(src, dst.at[0], o_sem.at[i])
        for i, (src, dst) in enumerate(((gwg, gwg_o), (gwu, gwu_o), (gwd, gwd_o)))
    ]
    for c in stores:
        c.start()

    sends = []
    lane128 = lax.broadcasted_iota(jnp.int32, (2 * TOK, 128), 1)
    for s in range(STEPS):
        za, zb = pair(s)
        bulk(pr_r.at[s]).wait()
        g = rret[s, 0:ROWS, :]
        o = rret[s, ROWS : 2 * ROWS, :]
        one = mats[s, 0 : 2 * TOK, :]
        tg = dot(one, g, 1, 0)
        mx = dot(mats[s, 2 * TOK : 4 * TOK, :], o, 1, 0) + dot(mats[s, 4 * TOK : 6 * TOK, :], o, 1, 0)
        inner = dot(both(gath, za, zb, TOK, TOK), o, 1, 1) * one.astype(F32)
        info = both(meta, za, zb, 0, TOK)
        quot = jnp.zeros((2 * TOK, 128), F32)
        for k in range(TOP):
            hit = info[:, k : k + 1] == ids
            v = jnp.sum(jnp.where(hit, inner, 0.0), axis=1, keepdims=True)
            quot = jnp.where(lane128 == k, v, quot)
        for i, zz in ((0, za), (1, zb)):
            part = slice(i * TOK, (i + 1) * TOK)
            if OFFSETS[s][i] == 0:
                zrx[z, 0:TOK, :] = mx[part, :].astype(BF)
                zrx[z, TOK : 2 * TOK, :] = tg[part, :].astype(BF)
                zqr[z] = quot[part, :]
                continue
            zs[s, i, 0:TOK, :] = mx[part, :].astype(BF)
            zs[s, i, TOK : 2 * TOK, :] = tg[part, :].astype(BF)
            zq[s, i] = quot[part, :]
            for src, dst, ss, rs in ((zs, zrx, zr_s, zr_r), (zq, zqr, zq_s, zq_r)):
                c = pltpu.make_async_remote_copy(
                    src_ref=src.at[s, i],
                    dst_ref=dst.at[z],
                    send_sem=ss.at[s, i],
                    recv_sem=rs.at[z],
                    device_id=at_z(OFFSETS[s][i]),
                    device_id_type=MESH,
                )
                c.start()
                sends.append(c)

    @pl.loop(1, NZ)
    def _(r):
        zz = (z + r) % NZ
        pltpu.make_async_copy(zrx.at[zz], zrx.at[zz], zr_r.at[zz]).wait()
        pltpu.make_async_copy(zqr.at[zz], zqr.at[zz], zq_r.at[zz]).wait()

    total = zrx[0].astype(F32)
    quot = zqr[0]
    for i in range(1, NZ):
        total += zrx[i].astype(F32)
        quot += zqr[i]
    fin[...] = total.astype(BF)
    finq[...] = quot
    last = [
        pltpu.make_async_remote_copy(
            src_ref=src, dst_ref=dst, send_sem=f_s.at[i], recv_sem=f_r.at[i],
            device_id=partner, device_id_type=MESH,
        )
        for i, (src, dst) in enumerate(((fin, finr), (finq, finqr)))
    ]
    for c in last:
        c.start()
    mixed_o[:, pl.ds(hs, HALF)] = fin[0:TOK, :]
    tgrad_o[:, pl.ds(hs, HALF)] = fin[TOK : 2 * TOK, :]
    for c in last:
        c.wait()
    mixed_o[:, pl.ds(ho, HALF)] = finr[0:TOK, :]
    tgrad_o[:, pl.ds(ho, HALF)] = finr[TOK : 2 * TOK, :]
    gg_o[...] = (quot + finqr[...])[:, 0:TOP]

    for c in hops:
        c.wait_send()
    for s in range(STEPS):
        bulk(pd_s.at[s]).wait()
        bulk(pr_s.at[s]).wait()
    for c in sends:
        c.wait_send()
    for c in stores:
        c.wait()


def body(tokens, routes, gates, cotangent, w_gate, w_up, w_down):
    vm = pl.BlockSpec(memory_space=pltpu.VMEM)
    hbm = pl.BlockSpec(memory_space=pl.ANY)
    dma = pltpu.SemaphoreType.DMA
    return pl.pallas_call(
        kernel,
        out_shape=(
            jax.ShapeDtypeStruct((TOK, D), BF),
            jax.ShapeDtypeStruct((TOK, D), BF),
            jax.ShapeDtypeStruct((TOK, TOP), F32),
            jax.ShapeDtypeStruct((1, D, HID), BF),
            jax.ShapeDtypeStruct((1, D, HID), BF),
            jax.ShapeDtypeStruct((1, HID, D), BF),
        ),
        in_specs=[vm] * 4 + [hbm] * 3,
        out_specs=(vm, vm, vm, hbm, hbm, hbm),
        scratch_shapes=[
            pltpu.VMEM((NZ, 2 * TOK, HALF), BF),
            pltpu.VMEM((NZ, TOK, 128), F32),
            pltpu.VMEM((STEPS, 6 * TOK, ROWS), BF),
            pltpu.VMEM((STEPS, 2 * ROWS, HALF), BF),
            pltpu.VMEM((STEPS * ROWS, D), BF),
            pltpu.VMEM((STEPS * ROWS, D), BF),
            pltpu.VMEM((D, HID), BF),
            pltpu.VMEM((D, HID), BF),
            pltpu.VMEM((HID, D), BF),
            pltpu.VMEM((2 * ROWS, HALF), F32),
            pltpu.VMEM((STEPS, 2 * ROWS, HALF), BF),
            pltpu.VMEM((STEPS, 2 * ROWS, HALF), BF),
            pltpu.VMEM((STEPS, 2 * ROWS, HALF), BF),
            pltpu.VMEM((STEPS, 2 * ROWS, HALF), BF),
            pltpu.VMEM((STEPS, 2, 2 * TOK, HALF), BF),
            pltpu.VMEM((STEPS, 2, TOK, 128), F32),
            pltpu.VMEM((NZ, 2 * TOK, HALF), BF),
            pltpu.VMEM((NZ, TOK, 128), F32),
            pltpu.VMEM((2 * TOK, HALF), BF),
            pltpu.VMEM((2 * TOK, HALF), BF),
            pltpu.VMEM((TOK, 128), F32),
            pltpu.VMEM((TOK, 128), F32),
            pltpu.VMEM((STEPS * ROWS, HID), BF),
            pltpu.VMEM((STEPS * ROWS, 2 * HID), BF),
            pltpu.VMEM((D, HID), BF),
            pltpu.VMEM((D, HID), BF),
            pltpu.VMEM((HID, D), BF),
            dma((3,)),
            dma((3, 2, 4)),
            dma((3, 2, 4)),
            dma((STEPS,)),
            dma((STEPS,)),
            dma((STEPS, 2)),
            dma((STEPS, 2)),
            dma((STEPS,)),
            dma((STEPS,)),
            dma((STEPS,)),
            dma((STEPS,)),
            dma((STEPS, 2)),
            dma((NZ,)),
            dma((STEPS, 2)),
            dma((NZ,)),
            dma((2,)),
            dma((2,)),
            dma((3,)),
        ],
        compiler_params=pltpu.CompilerParams(
            collective_id=0, has_side_effects=True, vmem_limit_bytes=60 << 20
        ),
        name="moe",
    )(tokens, cotangent, routes, gates, w_gate, w_up, w_down)


def solution(mesh):
    placed = (
        P("expert", None),
        P("expert", None),
        P("expert", None),
        P("expert", None),
        P("expert", None, "half"),
        P("expert", None, "half"),
        P("expert", "half", None),
    )
    return jax.shard_map(
        body,
        mesh=mesh,
        in_specs=placed,
        out_specs=(
            P("expert", None),
            P("expert", None),
            P("expert", None),
            P("expert", None, "half"),
            P("expert", None, "half"),
            P("expert", "half", None),
        ),
        check_vma=False,
    )
```

time: 413 us -> 165 us (0.40)
  blocking collectives: 216 us -> 0 us
  Pallas kernels: 0 us -> 149 us
  waiting for transfers between devices: 66.1 us -> 0 us
  local copies, waits for them, and re-layouts: 49.8 us -> 13.5 us
  matrix products: 32.3 us -> 0 us
  other arithmetic: 28 us -> 0 us
  between operations: 14.5 us -> 0.65 us
    all_to_all x2 -> x0, blocking collectives: 216 us -> none  [side_by_side(): lax.all_to_all(both, axis, split_axis=split_dim, concat_axis=concat_dim,...]
    pallas_call x0 -> x1, Pallas kernels: none -> 149 us  [body(): pl.pallas_call(kernel, out_shape=(jax.ShapeDtypeStruct((TOK, D), BF), jax...]
    gather x5 -> x0, local copies, waits for them, and re-layouts: 35.3 us -> none  [the longest x1 8.35 us: body(): out_home.reshape(experts * capacity, features)[target]]
    all_gather x2 -> x0, waiting for transfers between devices: 33.4 us -> none  [sent_together(): lax.all_gather(both, axis, axis=dim, tiled=True)]
    reduce_scatter x1 -> x0, waiting for transfers between devices: 32.6 us -> none  [sent_together_2(): lax.psum_scatter(both, axis, scatter_dimension=dim, tiled=True)]
    dot_general x9 -> x0, matrix products: 32.3 us -> none  [the longest x6 24.7 us: contract(): lax.dot_general(left, right, (((left_dim,), (right_dim,)), ((), ())), pre...]
    concatenate x5 -> x0, other arithmetic: 12.1 us -> none  [the longest x1 6.18 us: sent_together_2(): both = jnp.concatenate(arrays, axis=along)]
    unnamed x36 -> x11, local copies, waits for them, and re-layouts: 3.97 us -> 12.1 us
  transfers between devices with their start and end apart: 3 -> 0, of which waited for: 3 -> 0; matrix products, arithmetic and copies ran while one was open for 4% -> 0% of each run, Pallas kernels for 0% -> 0%
where the time goes in v1:
time: 165 us; the launch traced here: 163 us
  Pallas kernels  149 us (90%)
  local copies, waits for them, and re-layouts  13.5 us (8%)
    pallas_call x1, Pallas kernels, body(): pl.pallas_call(kernel, out_shape=(jax.ShapeDtypeStruct((TOK, D), BF), jax...  149 us
    unnamed x11, local copies, waits for them, and re-layouts  12.1 us

profile of v1, /device:TPU:1, one launch (start us, length us, event | category | flops | bytes accessed | tf_op | source)
XLA Modules:
  0.0 163.4 jit_solution(5646335217221676873)
XLA Ops:
  0.6 1.4 copy.13.routes
  2.0 1.4 copy.14.gates
  3.4 149.2 %moe.1 = (bf16[64,2048]{1,0:T(8,128)(2,1)}, bf16[64,2048]{1,0:T(8,128)(2,1)}, f32[64,8]{1,0:T(8,128)}, bf16[1,2048,384]{2,1,0:T(8,128)(2,1)}, bf16[1,2048,384]{2...) custom-call(bf16[64,2048]{1,0:T(8,128)(2,1)} %tok.1, bf16[64,2048]{1,0:T(8,128)(2,1)} %cot.1, s32[64,8]{1,0:T(8,128)} %copy.13.routes, ...), custom_call_target="tpu_custom_call" | custom-call | tf_op jit(solution)/shard_map/moe/pallas_call | solution.py:358
  152.6 1.4 copy.15
  154.1 1.7 %copy.21 = bf16[64,2048]{1,0:T(8,128)(2,1)} copy(bf16[64,2048]{1,0:T(8,128)(2,1)} %get-tuple-element.18) | data formatting | bytes 524288
  155.7 1.7 %copy.22 = bf16[64,2048]{1,0:T(8,128)(2,1)} copy(bf16[64,2048]{1,0:T(8,128)(2,1)} %get-tuple-element.19) | data formatting | bytes 524288
  157.4 0.0 copy-start.1
  157.4 2.8 %copy.23 = bf16[1,2048,384]{2,1,0:T(8,128)(2,1)} copy(bf16[1,2048,384]{2,1,0:T(8,128)(2,1)} %get-tuple-element.21) | data formatting | bytes 3145728
  160.2 0.0 copy-done.1
  160.2 0.0 copy-start
  160.2 1.1 copy.24
  161.4 0.8 copy-done
  162.2 1.1 copy.25
Async XLA Ops:
  157.4 2.8 %copy-start.1 = (bf16[1,2048,384]{2,1,0:T(8,128)(2,1)S(1)}, bf16[1,2048,384]{2,1,0:T(8,128)(2,1)}, u32[]{:S(2)}) copy-start(bf16[1,2048,384]{2,1,0:T(8,128)(2,1)} %get-tuple-element.22) | copy-start | bytes 4718596
  160.2 2.0 %copy-start = (bf16[1,384,2048]{2,1,0:T(8,128)(2,1)S(1)}, bf16[1,384,2048]{2,1,0:T(8,128)(2,1)}, u32[]{:S(2)}) copy-start(bf16[1,384,2048]{2,1,0:T(8,128)(2,1)} %get-tuple-element.23) | copy-start | bytes 4718596

commit v2 on v0

v2 whole, which is shorter than its diff:
```python
import jax
import jax.numpy as jnp
from jax import lax
from jax.experimental import pallas as pl
from jax.experimental.pallas import tpu as pltpu
from jax.sharding import PartitionSpec as P

MESH = pl.DeviceIdType.MESH
NX, NZ, NY = 4, 8, 4
PLANE = NX * NY
TOK = 64
D = 2048
HALF = D // 2
HID = 384
TOP = 8
CAP = 8
ROWS = PLANE * 2 * CAP
FAR_FIRST = (10, 6, 9, 11, 14, 5, 7, 13, 15, 2, 8, 1, 4, 3, 12)
BF = jnp.bfloat16
F32 = jnp.float32


def dot(a, b, ca, cb):
    return lax.dot_general(a, b, (((ca,), (cb,)), ((), ())), preferred_element_type=F32)


def kernel(
    tok, cot, routes, gates, wg_h, wu_h, wd_h,
    mixed_o, tgrad_o, gg_o, gwg_o, gwu_o, gwd_o,
    gath, meta, mats, sel, recv, wg, wu, wd, own, psend, precv, ret, rret,
    zs, zq, zx, zqx, fin, finr, finq, finqr, hid, dgu, gwg, gwu, gwd,
    w_sem, zt_s, zt_r, pd_s, pd_r, cx_s, cx_r, px_s, px_r, pr_s, pr_r,
    zr_s, zr_r, zq_s, zq_r, f_s, f_r, o_sem,
):
    e = lax.axis_index("expert")
    h = lax.axis_index("half")
    x, z, y = e // (NZ * NY), (e // NY) % NZ, e % NY
    me = x * NY + y
    mine = pl.ds(pl.multiple_of(h * HALF, HALF), HALF)
    other = pl.ds(pl.multiple_of((1 - h) * HALF, HALF), HALF)

    def at_z(dz):
        return ((x * NZ + (z + dz) % NZ) * NY + y, h)

    def in_plane(r):
        xx = (x + r // NY) % NX
        yy = (y + r % NY) % NY
        return ((xx * NZ + z) * NY + yy, h), xx * NY + yy

    partner = (e, 1 - h)

    def remote(src, dst, ss, rs, dev):
        return pltpu.make_async_remote_copy(
            src_ref=src, dst_ref=dst, send_sem=ss, recv_sem=rs, device_id=dev, device_id_type=MESH
        )

    loads = [
        pltpu.make_async_copy(src.at[0], dst, w_sem.at[i])
        for i, (src, dst) in enumerate(((wg_h, wg), (wu_h, wu), (wd_h, wd)))
    ]
    for c in loads:
        c.start()

    barrier = pltpu.get_barrier_semaphore()
    for r in range(1, PLANE):
        pl.semaphore_signal(barrier, inc=1, device_id=in_plane(r)[0], device_id_type=MESH)
    for r in range(1, NZ):
        pl.semaphore_signal(barrier, inc=1, device_id=at_z(r), device_id_type=MESH)
    pl.semaphore_signal(barrier, inc=1, device_id=partner, device_id_type=MESH)

    gath[z, 0:TOK, :] = tok[:, mine]
    gath[z, TOK : 2 * TOK, :] = cot[:, mine]
    flat = jnp.concatenate([routes[...].astype(F32), gates[...]], axis=0)
    flat = jnp.concatenate([flat, jnp.zeros((112, TOK), F32)], axis=0)
    meta[z] = flat.T

    lane = lax.broadcasted_iota(jnp.int32, (TOK, ROWS), 1)
    expert = lane // (2 * CAP)
    ids = ((expert // NY * NZ + z) * NY + expert % NY).astype(F32)
    slot = (lane % CAP).astype(F32)
    kind = ((lane // CAP) % 2).astype(F32)

    def select(s):
        zz = (z + s) % NZ
        info = meta[zz]
        named = jnp.zeros((TOK, ROWS), F32)
        weight = jnp.zeros((TOK, ROWS), F32)
        for k in range(TOP):
            hit = info[:, k : k + 1] == ids
            named = jnp.where(hit, 1.0, named)
            weight = jnp.where(hit, info[:, TOP + k : TOP + k + 1], weight)
        r0 = lax.broadcasted_iota(jnp.int32, (TOK, TOK), 0)
        r1 = lax.broadcasted_iota(jnp.int32, (TOK, TOK), 1)
        before = jnp.where(r1 < r0, 1.0, 0.0).astype(BF)
        placed = dot(before, named.astype(BF), 1, 0)
        one = jnp.where(placed == slot, named, 0.0)
        out_one = one * kind
        weight = out_one * weight
        high = weight.astype(BF)
        low = (weight - high.astype(F32)).astype(BF)
        mats[s, 0:TOK, :] = (one - out_one).astype(BF)
        mats[s, TOK : 2 * TOK, :] = high
        mats[s, 2 * TOK : 3 * TOK, :] = low
        mats[s, 3 * TOK : 4 * TOK, :] = out_one.astype(BF)
        source = jnp.concatenate([gath[zz], gath[zz, TOK : 2 * TOK, :]], axis=0)
        sel[s] = dot(mats[s, 0 : 3 * TOK, :], source, 0, 0).astype(BF)

    select(0)
    pl.semaphore_wait(barrier, PLANE - 1 + NZ - 1 + 1)

    def hop(stream, way, d, src_z):
        ref = meta.at[src_z] if stream == 2 else gath.at[src_z, pl.ds(stream * TOK, TOK)]
        return remote(
            ref, ref, zt_s.at[stream, way, d - 1], zt_r.at[stream, way, d - 1],
            at_z(1 if way == 0 else NZ - 1),
        )

    reach = ((4, 3), (3, 4), (4, 3))
    hops = []
    for stream in (2, 0, 1):
        for way in (1, 0):
            c = hop(stream, way, 1, z)
            c.start()
            hops.append(c)

    def arrive(d):
        for stream in (2, 0, 1):
            for way in (1, 0):
                if d <= reach[stream][way]:
                    src = (z + NZ - d) % NZ if way == 0 else (z + d) % NZ
                    hop(stream, way, d, src).wait_recv()
                    if d + 1 <= reach[stream][way]:
                        c = hop(stream, way, d + 1, src)
                        c.start()
                        hops.append(c)

    def block(p):
        return pl.ds(pl.multiple_of(p * 2 * CAP, 2 * CAP), 2 * CAP)

    def dispatch(s):
        for r in FAR_FIRST:
            dev, p = in_plane(r)
            remote(
                sel.at[s, block(p)], recv.at[s, block(me), mine], pd_s.at[s], pd_r.at[s], dev
            ).start()
        recv[s, block(me), mine] = sel[s, block(me), :]

    def bulk(sem):
        blocks = sel.at[0, pl.ds(0, ROWS - 2 * CAP)]
        pltpu.make_async_copy(blocks, blocks, sem).wait()

    dispatch(0)
    for s in range(1, NZ):
        if s <= 4:
            arrive(s)
        select(s)
        dispatch(s)

    for c in loads:
        c.wait()

    def exchange(s):
        return remote(
            recv.at[s, :, mine], recv.at[s, :, mine], cx_s.at[s], cx_r.at[s], partner
        )

    def partial(s):
        return remote(psend.at[s % 2], precv.at[s % 4], px_s.at[s], px_r.at[s], partner)

    half = ROWS // 2

    def expert_step(s):
        at = pl.ds(pl.multiple_of(s * half, half), half)
        for q in range(4):
            f = slice(q * 512, (q + 1) * 512)
            v = recv[s, :, f].astype(F32).reshape(PLANE, 2, CAP, 512)
            recv[s, 0:half, f] = v[:, 0].reshape(half, 512).astype(BF)
            recv[s, half:ROWS, f] = v[:, 1].reshape(half, 512).astype(BF)
        r = recv[s, 0:half, :]
        pre_gate = dot(r, wg[...], 1, 0)
        pre_up = dot(r, wu[...], 1, 0)
        back = dot(recv[s, half:ROWS, :], wd[...], 1, 1)
        sigma = jax.nn.sigmoid(pre_gate)
        hidden = (pre_gate * sigma * pre_up).astype(BF)
        d_up = (back * pre_gate * sigma).astype(BF)
        d_gate = (back * pre_up * sigma * (1.0 + pre_gate * (1.0 - sigma))).astype(BF)
        hid[at, :] = hidden
        dgu[at, 0:HID] = d_gate
        dgu[at, HID : 2 * HID] = d_up
        p = s % 2
        psend[p, 0:half, :] = (dot(d_gate, wg[other, :], 1, 1) + dot(d_up, wu[other, :], 1, 1)).astype(BF)
        psend[p, half:ROWS, :] = dot(hidden, wd[:, other], 1, 0).astype(BF)
        partial(s).start()
        own[p, 0:half, :] = dot(d_gate, wg[mine, :], 1, 1) + dot(d_up, wu[mine, :], 1, 1)
        own[p, half:ROWS, :] = dot(hidden, wd[:, mine], 1, 0)

    def go_home(s):
        partial(s).wait()
        v = own[s % 2] + precv[s % 4].astype(F32)
        v = jnp.concatenate(
            [v[0:half].reshape(PLANE, 1, CAP, HALF), v[half:ROWS].reshape(PLANE, 1, CAP, HALF)], axis=1
        )
        ret[s] = v.reshape(ROWS, HALF).astype(BF)
        for k in FAR_FIRST:
            dev, p = in_plane(k)
            remote(ret.at[s, block(p)], rret.at[s, block(me)], pr_s.at[s], pr_r.at[s], dev).start()
        rret[s, block(me), :] = ret[s, block(me), :]

    lane128 = lax.broadcasted_iota(jnp.int32, (TOK, 128), 1)

    def leave(s):
        dz = s + (s // 4) * (NZ - 1 - s)
        return remote(zs.at[s], zx.at[s], zr_s.at[s], zr_r.at[s], at_z(dz))

    def leave_inner(s):
        return remote(zq.at[s], zqx.at[s], zq_s.at[s], zq_r.at[s], at_z(s))

    def gather_home(s, chained=False):
        zz = (z + s) % NZ
        bulk(pr_r.at[s])
        r = rret[s]
        sums = dot(mats[s, 0 : 3 * TOK, :], r, 1, 0)
        mx = sums[TOK : 2 * TOK] + sums[2 * TOK : 3 * TOK]
        tg = sums[0:TOK]
        inner = dot(gath[zz, TOK : 2 * TOK, :], r, 1, 1) * mats[s, 3 * TOK : 4 * TOK, :].astype(F32)
        if chained:
            leave(s - 1).wait_recv()
            mx += zx[s - 1, 0:TOK, :].astype(F32)
            tg += zx[s - 1, TOK : 2 * TOK, :].astype(F32)
        zs[s, 0:TOK, :] = mx.astype(BF)
        zs[s, TOK : 2 * TOK, :] = tg.astype(BF)

        @pl.when(s > 0)
        def _():
            leave(s).start()

        info = meta[zz]
        quot = jnp.zeros((TOK, 128), F32)
        for k in range(TOP):
            hit = info[:, k : k + 1] == ids
            v = jnp.sum(jnp.where(hit, inner, 0.0), axis=1, keepdims=True)
            quot = jnp.where(lane128 == k, v, quot)
        zq[s] = jnp.concatenate([quot, jnp.zeros((128 - TOK, 128), F32)], axis=0).T[0:TOP, :]

        @pl.when(s > 0)
        def _():
            leave_inner(s).start()

    bulk(pd_r.at[0])
    exchange(0).start()

    @pl.loop(0, NZ)
    def _(s):
        @pl.when(s < NZ - 1)
        def _():
            bulk(pd_r.at[s + 1])
            exchange(s + 1).start()

        exchange(s).wait()
        expert_step(s)

        @pl.when(s > 0)
        def _():
            go_home(s - 1)

        @pl.when(s > 2)
        def _():
            gather_home(s - 3)

    go_home(NZ - 1)

    def weights(i):
        f = pl.ds(pl.multiple_of(i * 256, 256), 256)
        g = dot(recv[:, 0:half, f].reshape(NZ * half, 256), dgu[...], 0, 0)
        gwg[f, :] = g[:, 0:HID].astype(BF)
        gwu[f, :] = g[:, HID : 2 * HID].astype(BF)
        gwd[:, f] = dot(hid[...], recv[:, half:ROWS, f].reshape(NZ * half, 256), 0, 0).astype(BF)

    pl.loop(0, 4)(weights)
    gather_home(NZ - 3, chained=True)
    pl.loop(4, D // 256)(weights)
    stores = [
        pltpu.make_async_copy(src, dst.at[0], o_sem.at[i])
        for i, (src, dst) in enumerate(((gwg, gwg_o), (gwu, gwu_o), (gwd, gwd_o)))
    ]
    for c in stores:
        c.start()
    gather_home(NZ - 2, chained=True)
    gather_home(NZ - 1, chained=True)

    total = zs[0].astype(F32)
    quot = zq[0]
    for s in range(1, NZ):
        leave_inner(s).wait_recv()
        quot += zqx[s]
    for s in (1, 2, 3, NZ - 1):
        leave(s).wait_recv()
        total += zx[s].astype(F32)
    fin[...] = total.astype(BF)
    finq[...] = quot
    last = [
        remote(src, dst, f_s.at[i], f_r.at[i], partner)
        for i, (src, dst) in enumerate(((fin, finr), (finq, finqr)))
    ]
    for c in last:
        c.start()
    mixed_o[:, mine] = fin[0:TOK, :]
    tgrad_o[:, mine] = fin[TOK : 2 * TOK, :]
    for c in last:
        c.wait()
    mixed_o[:, other] = finr[0:TOK, :]
    tgrad_o[:, other] = finr[TOK : 2 * TOK, :]
    gg_o[...] = (quot + finqr[...])[:, 0:TOK]

    for c in hops:
        c.wait_send()
    for s in range(NZ):
        bulk(pd_s.at[s])
        bulk(pr_s.at[s])
        if s:
            leave(s).wait_send()
            leave_inner(s).wait_send()
    for c in stores:
        c.wait()


def place(*refs):
    src, dst, held, (sem_in, sem_out) = refs[0:6], refs[6:12], refs[12:18], refs[18:20]
    into = [pltpu.make_async_copy(src[i], held[i], sem_in.at[i]) for i in range(6)]
    out = [pltpu.make_async_copy(held[i], dst[i], sem_out.at[i]) for i in range(6)]
    for c in into:
        c.start()
    for a, b in zip(into, out):
        a.wait()
        b.start()
    for b in out:
        b.wait()


def body(tokens, routes, gates, cotangent, w_gate, w_up, w_down):
    vm = pl.BlockSpec(memory_space=pltpu.VMEM)
    hbm = pl.BlockSpec(memory_space=pl.ANY)
    dma = pltpu.SemaphoreType.DMA
    shapes = (
        jax.ShapeDtypeStruct((TOK, D), BF),
        jax.ShapeDtypeStruct((TOK, D), BF),
        jax.ShapeDtypeStruct((TOP, TOK), F32),
        jax.ShapeDtypeStruct((1, D, HID), BF),
        jax.ShapeDtypeStruct((1, D, HID), BF),
        jax.ShapeDtypeStruct((1, HID, D), BF),
    )
    outs = pl.pallas_call(
        kernel,
        out_shape=shapes,
        in_specs=[vm] * 4 + [hbm] * 3,
        out_specs=(vm, vm, vm, hbm, hbm, hbm),
        scratch_shapes=[
            pltpu.VMEM((NZ, 2 * TOK, HALF), BF),
            pltpu.VMEM((NZ, TOK, 128), F32),
            pltpu.VMEM((NZ, 4 * TOK, ROWS), BF),
            pltpu.VMEM((NZ, ROWS, HALF), BF),
            pltpu.VMEM((NZ, ROWS, D), BF),
            pltpu.VMEM((D, HID), BF),
            pltpu.VMEM((D, HID), BF),
            pltpu.VMEM((HID, D), BF),
            pltpu.VMEM((2, ROWS, HALF), F32),
            pltpu.VMEM((2, ROWS, HALF), BF),
            pltpu.VMEM((4, ROWS, HALF), BF),
            pltpu.VMEM((NZ, ROWS, HALF), BF),
            pltpu.VMEM((NZ, ROWS, HALF), BF),
            pltpu.VMEM((NZ, 2 * TOK, HALF), BF),
            pltpu.VMEM((NZ, TOP, 128), F32),
            pltpu.VMEM((NZ, 2 * TOK, HALF), BF),
            pltpu.VMEM((NZ, TOP, 128), F32),
            pltpu.VMEM((2 * TOK, HALF), BF),
            pltpu.VMEM((2 * TOK, HALF), BF),
            pltpu.VMEM((TOP, 128), F32),
            pltpu.VMEM((TOP, 128), F32),
            pltpu.VMEM((NZ * ROWS // 2, HID), BF),
            pltpu.VMEM((NZ * ROWS // 2, 2 * HID), BF),
            pltpu.VMEM((D, HID), BF),
            pltpu.VMEM((D, HID), BF),
            pltpu.VMEM((HID, D), BF),
            dma((3,)),
            dma((3, 2, 4)),
            dma((3, 2, 4)),
        ]
        + [dma((NZ,))] * 12
        + [dma((2,)), dma((2,)), dma((3,))],
        compiler_params=pltpu.CompilerParams(
            collective_id=0, has_side_effects=True, vmem_limit_bytes=60 << 20
        ),
        name="moe",
    )(tokens, cotangent, routes.T, gates.T, w_gate, w_up, w_down)
    outs = pl.pallas_call(
        place,
        out_shape=shapes,
        in_specs=[hbm] * 6,
        out_specs=[hbm] * 6,
        scratch_shapes=[pltpu.VMEM(o.shape, o.dtype) for o in shapes] + [dma((6,)), dma((6,))],
        compiler_params=pltpu.CompilerParams(vmem_limit_bytes=60 << 20),
        name="place",
    )(*outs)
    return (outs[0], outs[1], outs[2].T) + tuple(outs[3:])


def solution(mesh):
    placed = (
        P("expert", None),
        P("expert", None),
        P("expert", None),
        P("expert", None),
        P("expert", None, "half"),
        P("expert", None, "half"),
        P("expert", "half", None),
    )
    return jax.shard_map(
        body,
        mesh=mesh,
        in_specs=placed,
        out_specs=(
            P("expert", None),
            P("expert", None),
            P("expert", None),
            P("expert", None, "half"),
            P("expert", None, "half"),
            P("expert", "half", None),
        ),
        check_vma=False,
    )
```

time: 413 us -> 130 us (0.31); the launches traced: 407 us -> 130 us
  blocking collectives: 216 us -> 0 us
  Pallas kernels: 0 us -> 129 us
  waiting for transfers between devices: 66.1 us -> 0 us
  local copies, waits for them, and re-layouts: 49.8 us -> 0 us
  matrix products: 32.3 us -> 0 us
  other arithmetic: 28 us -> 0 us
  between operations: 14.5 us -> 0.64 us
    all_to_all x2 -> x0, blocking collectives: 216 us -> none  [side_by_side(): lax.all_to_all(both, axis, split_axis=split_dim, concat_axis=concat_dim,...]
    pallas_call x0 -> x2, Pallas kernels: none -> 129 us  [the longest x1 125 us: body(): pl.pallas_call(kernel, out_shape=shapes, in_specs=[vm] * 4 + [hbm] * 3, o...]
    gather x5 -> x0, local copies, waits for them, and re-layouts: 35.3 us -> none  [the longest x1 8.35 us: body(): out_home.reshape(experts * capacity, features)[target]]
    all_gather x2 -> x0, waiting for transfers between devices: 33.4 us -> none  [sent_together(): lax.all_gather(both, axis, axis=dim, tiled=True)]
    reduce_scatter x1 -> x0, waiting for transfers between devices: 32.6 us -> none  [sent_together_2(): lax.psum_scatter(both, axis, scatter_dimension=dim, tiled=True)]
    dot_general x9 -> x0, matrix products: 32.3 us -> none  [the longest x6 24.7 us: contract(): lax.dot_general(left, right, (((left_dim,), (right_dim,)), ((), ())), pre...]
    concatenate x5 -> x0, other arithmetic: 12.1 us -> none  [the longest x1 6.18 us: sent_together_2(): both = jnp.concatenate(arrays, axis=along)]
    reduce_sum x3 -> x0, other arithmetic: 7.91 us -> none  [the longest x1 3.97 us: body(): jnp.sum(cotangent.astype(jnp.float32)[:, None, :] * out_float, axis=2)]
  transfers between devices with their start and end apart: 3 -> 0, of which waited for: 3 -> 0; matrix products, arithmetic and copies ran while one was open for 4% -> 0% of each run, Pallas kernels for 0% -> 0%
where the time goes in v2:
time: 130 us
  Pallas kernels  129 us (99%)
    pallas_call x1, Pallas kernels, body(): pl.pallas_call(kernel, out_shape=shapes, in_specs=[vm] * 4 + [hbm] * 3, o...  125 us
    pallas_call x1, Pallas kernels, body(): pl.pallas_call(place, out_shape=shapes, in_specs=[hbm] * 6, out_specs=[hb...  4.38 us

profile of v2, /device:TPU:1, one launch (start us, length us, event | category | flops | bytes accessed | tf_op | source)
XLA Modules:
  0.0 129.5 jit_solution(4740253559526098689)
XLA Ops:
  0.6 124.5 %moe.1 = (bf16[64,2048]{1,0:T(8,128)(2,1)}, bf16[64,2048]{1,0:T(8,128)(2,1)}, f32[8,64]{1,0:T(8,128)}, bf16[1,2048,384]{2,1,0:T(8,128)(2,1)}, bf16[1,2048,384]{2...) custom-call(bf16[64,2048]{1,0:T(8,128)(2,1)} %tok.1, bf16[64,2048]{1,0:T(8,128)(2,1)} %cot.1, s32[8,64]{1,0:T(8,128)} %bitcast.3, ...), custom_call_target="tpu_custom_call" | custom-call | tf_op jit(solution)/shard_map/moe/pallas_call | solution.py:352
  125.2 4.4 %place.1 = (bf16[64,2048]{1,0:T(8,128)(2,1)}, bf16[64,2048]{1,0:T(8,128)(2,1)}, f32[8,64]{1,0:T(8,128)}, bf16[1,2048,384]{2,1,0:T(8,128)(2,1)}, bf16[1,2048,384]...) custom-call(bf16[64,2048]{1,0:T(8,128)(2,1)} %get-tuple-element.18.refs_0_, bf16[64,2048]{1,0:T(8,128)(2,1)} %get-tuple-element.19.refs_1_, ...), custom_call_target="tpu_custom_call" | custom-call | tf_op jit(solution)/shard_map/place/pallas_call | solution.py:395

commit v3 on v2

--- a/solution.py
+++ b/solution.py
@@ -27,9 +27,9 @@
 def kernel(
     tok, cot, routes, gates, wg_h, wu_h, wd_h,
     mixed_o, tgrad_o, gg_o, gwg_o, gwu_o, gwd_o,
-    gath, meta, mats, sel, recv, wg, wu, wd, own, psend, precv, ret, rret,
+    routes_v, gates_v, gath, meta, mats, sel, recv, wg, wu, wd, own, psend, precv, ret, rret,
     zs, zq, zx, zqx, fin, finr, finq, finqr, hid, dgu, gwg, gwu, gwd,
-    w_sem, zt_s, zt_r, pd_s, pd_r, cx_s, cx_r, px_s, px_r, pr_s, pr_r,
+    i_sem, w_sem, zt_s, zt_r, pd_s, pd_r, cx_s, cx_r, px_s, px_r, pr_s, pr_r,
     zr_s, zr_r, zq_s, zq_r, f_s, f_r, o_sem,
 ):
     e = lax.axis_index("expert")
@@ -54,6 +54,14 @@
             src_ref=src, dst_ref=dst, send_sem=ss, recv_sem=rs, device_id=dev, device_id_type=MESH
         )
 
+    firsts = [
+        pltpu.make_async_copy(tok.at[:, mine], gath.at[z, pl.ds(0, TOK)], i_sem.at[0]),
+        pltpu.make_async_copy(cot.at[:, mine], gath.at[z, pl.ds(TOK, TOK)], i_sem.at[1]),
+        pltpu.make_async_copy(routes, routes_v, i_sem.at[2]),
+        pltpu.make_async_copy(gates, gates_v, i_sem.at[3]),
+    ]
+    for c in firsts:
+        c.start()
     loads = [
         pltpu.make_async_copy(src.at[0], dst, w_sem.at[i])
         for i, (src, dst) in enumerate(((wg_h, wg), (wu_h, wu), (wd_h, wd)))
@@ -68,9 +76,9 @@
         pl.semaphore_signal(barrier, inc=1, device_id=at_z(r), device_id_type=MESH)
     pl.semaphore_signal(barrier, inc=1, device_id=partner, device_id_type=MESH)
 
-    gath[z, 0:TOK, :] = tok[:, mine]
-    gath[z, TOK : 2 * TOK, :] = cot[:, mine]
-    flat = jnp.concatenate([routes[...].astype(F32), gates[...]], axis=0)
+    for c in firsts:
+        c.wait()
+    flat = jnp.concatenate([routes_v[...].astype(F32), gates_v[...]], axis=0)
     flat = jnp.concatenate([flat, jnp.zeros((112, TOK), F32)], axis=0)
     meta[z] = flat.T
 
@@ -164,12 +172,16 @@
             recv.at[s, :, mine], recv.at[s, :, mine], cx_s.at[s], cx_r.at[s], partner
         )
 
-    def partial(s):
-        return remote(psend.at[s % 2], precv.at[s % 4], px_s.at[s], px_r.at[s], partner)
+    def turn(i):
+        return (i + 1) % NZ
+
+    def partial(i):
+        return remote(psend.at[i % 2], precv.at[i % 4], px_s.at[i], px_r.at[i], partner)
 
     half = ROWS // 2
 
-    def expert_step(s):
+    def expert_step(i):
+        s = turn(i)
         at = pl.ds(pl.multiple_of(s * half, half), half)
         for q in range(4):
             f = slice(q * 512, (q + 1) * 512)
@@ -187,16 +199,17 @@
         hid[at, :] = hidden
         dgu[at, 0:HID] = d_gate
         dgu[at, HID : 2 * HID] = d_up
-        p = s % 2
+        p = i % 2
         psend[p, 0:half, :] = (dot(d_gate, wg[other, :], 1, 1) + dot(d_up, wu[other, :], 1, 1)).astype(BF)
         psend[p, half:ROWS, :] = dot(hidden, wd[:, other], 1, 0).astype(BF)
-        partial(s).start()
+        partial(i).start()
         own[p, 0:half, :] = dot(d_gate, wg[mine, :], 1, 1) + dot(d_up, wu[mine, :], 1, 1)
         own[p, half:ROWS, :] = dot(hidden, wd[:, mine], 1, 0)
 
-    def go_home(s):
-        partial(s).wait()
-        v = own[s % 2] + precv[s % 4].astype(F32)
+    def go_home(i):
+        s = turn(i)
+        partial(i).wait()
+        v = own[i % 2] + precv[i % 4].astype(F32)
         v = jnp.concatenate(
             [v[0:half].reshape(PLANE, 1, CAP, HALF), v[half:ROWS].reshape(PLANE, 1, CAP, HALF)], axis=1
         )
@@ -215,57 +228,55 @@
     def leave_inner(s):
         return remote(zq.at[s], zqx.at[s], zq_s.at[s], zq_r.at[s], at_z(s))
 
+    def sums_of(s):
+        sums = dot(mats[s, 0 : 3 * TOK, :], rret[s], 1, 0)
+        return sums[TOK : 2 * TOK] + sums[2 * TOK : 3 * TOK], sums[0:TOK]
+
+    def inner_of(s):
+        zz = (z + s) % NZ
+        inner = dot(gath[zz, TOK : 2 * TOK, :], rret[s], 1, 1)
+        inner = inner * mats[s, 3 * TOK : 4 * TOK, :].astype(F32)
+        info = meta[zz]
+        quot = jnp.zeros((TOK, 128), F32)
+        for k in range(TOP):
+            hit = info[:, k : k + 1] == ids
+            v = jnp.sum(jnp.where(hit, inner, 0.0), axis=1, keepdims=True)
+            quot = jnp.where(lane128 == k, v, quot)
+        return jnp.concatenate([quot, jnp.zeros((128 - TOK, 128), F32)], axis=0).T[0:TOP, :]
+
     def gather_home(s, chained=False):
-        zz = (z + s) % NZ
         bulk(pr_r.at[s])
-        r = rret[s]
-        sums = dot(mats[s, 0 : 3 * TOK, :], r, 1, 0)
-        mx = sums[TOK : 2 * TOK] + sums[2 * TOK : 3 * TOK]
-        tg = sums[0:TOK]
-        inner = dot(gath[zz, TOK : 2 * TOK, :], r, 1, 1) * mats[s, 3 * TOK : 4 * TOK, :].astype(F32)
+        mx, tg = sums_of(s)
         if chained:
             leave(s - 1).wait_recv()
             mx += zx[s - 1, 0:TOK, :].astype(F32)
             tg += zx[s - 1, TOK : 2 * TOK, :].astype(F32)
         zs[s, 0:TOK, :] = mx.astype(BF)
         zs[s, TOK : 2 * TOK, :] = tg.astype(BF)
-
-        @pl.when(s > 0)
+        leave(s).start()
+        zq[s] = inner_of(s)
+        leave_inner(s).start()
+
+    bulk(pd_r.at[turn(0)])
+    exchange(turn(0)).start()
+
+    @pl.loop(0, NZ)
+    def _(i):
+        @pl.when(i < NZ - 1)
         def _():
-            leave(s).start()
-
-        info = meta[zz]
-        quot = jnp.zeros((TOK, 128), F32)
-        for k in range(TOP):
-            hit = info[:, k : k + 1] == ids
-            v = jnp.sum(jnp.where(hit, inner, 0.0), axis=1, keepdims=True)
-            quot = jnp.where(lane128 == k, v, quot)
-        zq[s] = jnp.concatenate([quot, jnp.zeros((128 - TOK, 128), F32)], axis=0).T[0:TOP, :]
-
-        @pl.when(s > 0)
+            bulk(pd_r.at[turn(i + 1)])
+            exchange(turn(i + 1)).start()
+
+        exchange(turn(i)).wait()
+        expert_step(i)
+
+        @pl.when(i > 0)
         def _():
-            leave_inner(s).start()
-
-    bulk(pd_r.at[0])
-    exchange(0).start()
-
-    @pl.loop(0, NZ)
-    def _(s):
-        @pl.when(s < NZ - 1)
+            go_home(i - 1)
+
+        @pl.when((i > 2) * (i < NZ - 1))
         def _():
-            bulk(pd_r.at[s + 1])
-            exchange(s + 1).start()
-
-        exchange(s).wait()
-        expert_step(s)
-
-        @pl.when(s > 0)
-        def _():
-            go_home(s - 1)
-
-        @pl.when(s > 2)
-        def _():
-            gather_home(s - 3)
+            gather_home(turn(i - 3))
 
     go_home(NZ - 1)
 
@@ -276,34 +287,41 @@
         gwu[f, :] = g[:, HID : 2 * HID].astype(BF)
         gwd[:, f] = dot(hid[...], recv[:, half:ROWS, f].reshape(NZ * half, 256), 0, 0).astype(BF)
 
-    pl.loop(0, 4)(weights)
-    gather_home(NZ - 3, chained=True)
-    pl.loop(4, D // 256)(weights)
+    pl.loop(0, 3)(weights)
+    gather_home(5, chained=True)
+    pl.loop(3, 6)(weights)
+    gather_home(6, chained=True)
+    pl.loop(6, D // 256)(weights)
     stores = [
         pltpu.make_async_copy(src, dst.at[0], o_sem.at[i])
         for i, (src, dst) in enumerate(((gwg, gwg_o), (gwu, gwu_o), (gwd, gwd_o)))
     ]
     for c in stores:
         c.start()
-    gather_home(NZ - 2, chained=True)
-    gather_home(NZ - 1, chained=True)
-
-    total = zs[0].astype(F32)
-    quot = zq[0]
+    gather_home(7, chained=True)
+
+    quot = jnp.zeros((TOP, 128), F32)
     for s in range(1, NZ):
         leave_inner(s).wait_recv()
         quot += zqx[s]
-    for s in (1, 2, 3, NZ - 1):
+    total = jnp.zeros((2 * TOK, HALF), F32)
+    for s in (1, 2, 3):
         leave(s).wait_recv()
         total += zx[s].astype(F32)
-    fin[...] = total.astype(BF)
-    finq[...] = quot
+    bulk(pr_r.at[0])
+    mx, tg = sums_of(0)
+    leave(NZ - 1).wait_recv()
+    total += zx[NZ - 1].astype(F32)
+    fin[0:TOK, :] = (total[0:TOK] + mx).astype(BF)
+    fin[TOK : 2 * TOK, :] = (total[TOK : 2 * TOK] + tg).astype(BF)
     last = [
         remote(src, dst, f_s.at[i], f_r.at[i], partner)
         for i, (src, dst) in enumerate(((fin, finr), (finq, finqr)))
     ]
-    for c in last:
-        c.start()
+    last[0].start()
+    quot += inner_of(0)
+    finq[...] = quot
+    last[1].start()
     mixed_o[:, mine] = fin[0:TOK, :]
     tgrad_o[:, mine] = fin[TOK : 2 * TOK, :]
     for c in last:
@@ -325,16 +343,13 @@
 
 
 def place(*refs):
-    src, dst, held, (sem_in, sem_out) = refs[0:6], refs[6:12], refs[12:18], refs[18:20]
-    into = [pltpu.make_async_copy(src[i], held[i], sem_in.at[i]) for i in range(6)]
-    out = [pltpu.make_async_copy(held[i], dst[i], sem_out.at[i]) for i in range(6)]
-    for c in into:
-        c.start()
-    for a, b in zip(into, out):
-        a.wait()
-        b.start()
-    for b in out:
-        b.wait()
+    src, dst, sem = refs[0:6], refs[6:12], refs[12]
+    copies = []
+    for i in range(6):
+        copies.append(pltpu.make_async_copy(src[i], dst[i], sem.at[i]))
+        copies[-1].start()
+    for c in copies:
+        c.wait()
 
 
 def body(tokens, routes, gates, cotangent, w_gate, w_up, w_down):
@@ -352,9 +367,11 @@
     outs = pl.pallas_call(
         kernel,
         out_shape=shapes,
-        in_specs=[vm] * 4 + [hbm] * 3,
+        in_specs=[pl.BlockSpec(memory_space=pltpu.HBM)] * 7,
         out_specs=(vm, vm, vm, hbm, hbm, hbm),
         scratch_shapes=[
+            pltpu.VMEM((TOP, TOK), jnp.int32),
+            pltpu.VMEM((TOP, TOK), F32),
             pltpu.VMEM((NZ, 2 * TOK, HALF), BF),
             pltpu.VMEM((NZ, TOK, 128), F32),
             pltpu.VMEM((NZ, 4 * TOK, ROWS), BF),
@@ -381,6 +398,7 @@
             pltpu.VMEM((D, HID), BF),
             pltpu.VMEM((D, HID), BF),
             pltpu.VMEM((HID, D), BF),
+            dma((4,)),
             dma((3,)),
             dma((3, 2, 4)),
             dma((3, 2, 4)),
@@ -388,19 +406,19 @@
         + [dma((NZ,))] * 12
         + [dma((2,)), dma((2,)), dma((3,))],
         compiler_params=pltpu.CompilerParams(
-            collective_id=0, has_side_effects=True, vmem_limit_bytes=60 << 20
+            collective_id=0, has_side_effects=True, vmem_limit_bytes=48 << 20
         ),
         name="moe",
-    )(tokens, cotangent, routes.T, gates.T, w_gate, w_up, w_down)
+    )(*[pltpu.with_memory_space_constraint(a, pltpu.HBM) for a in (tokens, cotangent, routes.T, gates.T, w_gate, w_up, w_down)])
     outs = pl.pallas_call(
         place,
         out_shape=shapes,
-        in_specs=[hbm] * 6,
+        in_specs=[vm] * 6,
         out_specs=[hbm] * 6,
-        scratch_shapes=[pltpu.VMEM(o.shape, o.dtype) for o in shapes] + [dma((6,)), dma((6,))],
-        compiler_params=pltpu.CompilerParams(vmem_limit_bytes=60 << 20),
+        scratch_shapes=[dma((6,))],
+        compiler_params=pltpu.CompilerParams(vmem_limit_bytes=8 << 20),
         name="place",
-    )(*outs)
+    )(*[pltpu.with_memory_space_constraint(o, pltpu.VMEM) for o in outs])
     return (outs[0], outs[1], outs[2].T) + tuple(outs[3:])
 
 

time: 130 us -> 124 us (0.954)
  Pallas kernels: 129 us -> 124 us
    pallas_call x2, Pallas kernels: 129 us -> 124 us  [the longest x1 121 us: body(): pl.pallas_call(kernel, out_shape=shapes, in_specs=[pl.BlockSpec(memory_sp...]
where the time goes in v3:
time: 124 us
  Pallas kernels  124 us (100%)
    pallas_call x1, Pallas kernels, body(): pl.pallas_call(kernel, out_shape=shapes, in_specs=[pl.BlockSpec(memory_sp...  121 us

profile of v3, /device:TPU:1, one launch (start us, length us, event | category | flops | bytes accessed | tf_op | source)
XLA Modules:
  0.0 124.3 jit_solution(17035717528237671144)
XLA Ops:
  0.6 121.1 %moe.1 = (bf16[64,2048]{1,0:T(8,128)(2,1)S(1)}, bf16[64,2048]{1,0:T(8,128)(2,1)S(1)}, f32[8,64]{1,0:T(8,128)S(1)}, bf16[1,2048,384]{2,1,0:T(8,128)(2,1)S(1)}, bf...) custom-call(bf16[64,2048]{1,0:T(8,128)(2,1)} %tok.1, bf16[64,2048]{1,0:T(8,128)(2,1)} %cot.1, ...), custom_call_target="tpu_custom_call" | custom-call | tf_op jit(solution)/shard_map/moe/pallas_call | solution.py:367
  121.8 2.4 %place.1 = (bf16[64,2048]{1,0:T(8,128)(2,1)}, bf16[64,2048]{1,0:T(8,128)(2,1)}, f32[8,64]{1,0:T(8,128)}, bf16[1,2048,384]{2,1,0:T(8,128)(2,1)}, bf16[1,2048,384]...) custom-call(bf16[64,2048]{1,0:T(8,128)(2,1)S(1)} %get-tuple-element.18.refs_0_, ...), custom_call_target="tpu_custom_call" | custom-call | tf_op jit(solution)/shard_map/place/pallas_call | solution.py:413

commit v4 on v3

--- a/solution.py
+++ b/solution.py
@@ -15,6 +15,7 @@
 TOP = 8
 CAP = 8
 ROWS = PLANE * 2 * CAP
+ORDER = (3, 4, 5, 2, 6, 1, 7, 0)
 FAR_FIRST = (10, 6, 9, 11, 14, 5, 7, 13, 15, 2, 8, 1, 4, 3, 12)
 BF = jnp.bfloat16
 F32 = jnp.float32
@@ -28,7 +29,7 @@
     tok, cot, routes, gates, wg_h, wu_h, wd_h,
     mixed_o, tgrad_o, gg_o, gwg_o, gwu_o, gwd_o,
     routes_v, gates_v, gath, meta, mats, sel, recv, wg, wu, wd, own, psend, precv, ret, rret,
-    zs, zq, zx, zqx, fin, finr, finq, finqr, hid, dgu, gwg, gwu, gwd,
+    acc, zs, zq, zx, zqx, fin, finr, finq, finqr, hid, dgu, gwg, gwu, gwd,
     i_sem, w_sem, zt_s, zt_r, pd_s, pd_r, cx_s, cx_r, px_s, px_r, pr_s, pr_r,
     zr_s, zr_r, zq_s, zq_r, f_s, f_r, o_sem,
 ):
@@ -173,7 +174,18 @@
         )
 
     def turn(i):
-        return (i + 1) % NZ
+        bits = (i % 2, (i // 2) % 2, i // 4)
+        total = 0
+        for m in range(NZ):
+            part = sum(
+                (-1) ** bin(m ^ k).count("1") * ORDER[k] for k in range(NZ) if k & m == k
+            )
+            if part:
+                for b in range(3):
+                    if m >> b & 1:
+                        part = part * bits[b]
+                total = total + part
+        return total
 
     def partial(i):
         return remote(psend.at[i % 2], precv.at[i % 4], px_s.at[i], px_r.at[i], partner)
@@ -244,15 +256,19 @@
             quot = jnp.where(lane128 == k, v, quot)
         return jnp.concatenate([quot, jnp.zeros((128 - TOK, 128), F32)], axis=0).T[0:TOP, :]
 
-    def gather_home(s, chained=False):
+    def gather_home(i, chained):
+        s = turn(i)
         bulk(pr_r.at[s])
         mx, tg = sums_of(s)
-        if chained:
+        acc[0:TOK, :] = mx
+        acc[TOK : 2 * TOK, :] = tg
+
+        @pl.when(chained)
+        def _():
             leave(s - 1).wait_recv()
-            mx += zx[s - 1, 0:TOK, :].astype(F32)
-            tg += zx[s - 1, TOK : 2 * TOK, :].astype(F32)
-        zs[s, 0:TOK, :] = mx.astype(BF)
-        zs[s, TOK : 2 * TOK, :] = tg.astype(BF)
+            acc[...] += zx[s - 1].astype(F32)
+
+        zs[s] = acc[...].astype(BF)
         leave(s).start()
         zq[s] = inner_of(s)
         leave_inner(s).start()
@@ -262,21 +278,21 @@
 
     @pl.loop(0, NZ)
     def _(i):
+        exchange(turn(i)).wait()
+        expert_step(i)
+
+        @pl.when(i > 0)
+        def _():
+            go_home(i - 1)
+
         @pl.when(i < NZ - 1)
         def _():
             bulk(pd_r.at[turn(i + 1)])
             exchange(turn(i + 1)).start()
 
-        exchange(turn(i)).wait()
-        expert_step(i)
-
-        @pl.when(i > 0)
+        @pl.when(i > 2)
         def _():
-            go_home(i - 1)
-
-        @pl.when((i > 2) * (i < NZ - 1))
-        def _():
-            gather_home(turn(i - 3))
+            gather_home(i - 3, (i == 5) | (i == 7))
 
     go_home(NZ - 1)
 
@@ -287,19 +303,16 @@
         gwu[f, :] = g[:, HID : 2 * HID].astype(BF)
         gwd[:, f] = dot(hid[...], recv[:, half:ROWS, f].reshape(NZ * half, 256), 0, 0).astype(BF)
 
-    pl.loop(0, 3)(weights)
-    gather_home(5, chained=True)
-    pl.loop(3, 6)(weights)
-    gather_home(6, chained=True)
-    pl.loop(6, D // 256)(weights)
+    gather_home(5, False)
+    pl.loop(0, 4)(weights)
+    gather_home(6, True)
+    pl.loop(4, D // 256)(weights)
     stores = [
         pltpu.make_async_copy(src, dst.at[0], o_sem.at[i])
         for i, (src, dst) in enumerate(((gwg, gwg_o), (gwu, gwu_o), (gwd, gwd_o)))
     ]
     for c in stores:
         c.start()
-    gather_home(7, chained=True)
-
     quot = jnp.zeros((TOP, 128), F32)
     for s in range(1, NZ):
         leave_inner(s).wait_recv()
@@ -385,6 +398,7 @@
             pltpu.VMEM((4, ROWS, HALF), BF),
             pltpu.VMEM((NZ, ROWS, HALF), BF),
             pltpu.VMEM((NZ, ROWS, HALF), BF),
+            pltpu.VMEM((2 * TOK, HALF), F32),
             pltpu.VMEM((NZ, 2 * TOK, HALF), BF),
             pltpu.VMEM((NZ, TOP, 128), F32),
             pltpu.VMEM((NZ, 2 * TOK, HALF), BF),

time: 124 us -> 119 us (0.960)
  Pallas kernels: 124 us -> 118 us
    pallas_call x1, Pallas kernels: 121 us -> 116 us  [body(): pl.pallas_call(kernel, out_shape=shapes, in_specs=[pl.BlockSpec(memory_sp...]
where the time goes in v4:
time: 119 us
  Pallas kernels  118 us (99%)
    pallas_call x1, Pallas kernels, body(): pl.pallas_call(kernel, out_shape=shapes, in_specs=[pl.BlockSpec(memory_sp...  116 us
    pallas_call x1, Pallas kernels, body(): pl.pallas_call(place, out_shape=shapes, in_specs=[vm] * 6, out_specs=[hbm...  2.41 us

profile of v4, /device:TPU:1, one launch (start us, length us, event | category | flops | bytes accessed | tf_op | source)
XLA Modules:
  0.0 118.7 jit_solution(3254777039152650326)
XLA Ops:
  0.6 115.7 %moe.1 = (bf16[64,2048]{1,0:T(8,128)(2,1)S(1)}, bf16[64,2048]{1,0:T(8,128)(2,1)S(1)}, f32[8,64]{1,0:T(8,128)S(1)}, bf16[1,2048,384]{2,1,0:T(8,128)(2,1)S(1)}, bf...) custom-call(bf16[64,2048]{1,0:T(8,128)(2,1)} %tok.1, bf16[64,2048]{1,0:T(8,128)(2,1)} %cot.1, ...), custom_call_target="tpu_custom_call" | custom-call | tf_op jit(solution)/shard_map/moe/pallas_call | solution.py:380
  116.3 2.4 %place.1 = (bf16[64,2048]{1,0:T(8,128)(2,1)}, bf16[64,2048]{1,0:T(8,128)(2,1)}, f32[8,64]{1,0:T(8,128)}, bf16[1,2048,384]{2,1,0:T(8,128)(2,1)}, bf16[1,2048,384]...) custom-call(bf16[64,2048]{1,0:T(8,128)(2,1)S(1)} %get-tuple-element.18.refs_0_, ...), custom_call_target="tpu_custom_call" | custom-call | tf_op jit(solution)/shard_map/place/pallas_call | solution.py:427

commit v5 on v4

--- a/solution.py
+++ b/solution.py
@@ -15,7 +15,8 @@
 TOP = 8
 CAP = 8
 ROWS = PLANE * 2 * CAP
-ORDER = (3, 4, 5, 2, 6, 1, 7, 0)
+OUTWARD = (0, 1, 7, 2, 3, 4, 5, 6)
+ORDER = (2, 3, 4, 5, 6, 1, 7, 0)
 FAR_FIRST = (10, 6, 9, 11, 14, 5, 7, 13, 15, 2, 8, 1, 4, 3, 12)
 BF = jnp.bfloat16
 F32 = jnp.float32
@@ -80,8 +81,7 @@
     for c in firsts:
         c.wait()
     flat = jnp.concatenate([routes_v[...].astype(F32), gates_v[...]], axis=0)
-    flat = jnp.concatenate([flat, jnp.zeros((112, TOK), F32)], axis=0)
-    meta[z] = flat.T
+    meta[z] = jnp.concatenate([flat, jnp.zeros((2 * TOP, 128 - TOK), F32)], axis=1)
 
     lane = lax.broadcasted_iota(jnp.int32, (TOK, ROWS), 1)
     expert = lane // (2 * CAP)
@@ -91,7 +91,7 @@
 
     def select(s):
         zz = (z + s) % NZ
-        info = meta[zz]
+        info = meta[zz].T[0:TOK]
         named = jnp.zeros((TOK, ROWS), F32)
         weight = jnp.zeros((TOK, ROWS), F32)
         for k in range(TOP):
@@ -114,7 +114,6 @@
         source = jnp.concatenate([gath[zz], gath[zz, TOK : 2 * TOK, :]], axis=0)
         sel[s] = dot(mats[s, 0 : 3 * TOK, :], source, 0, 0).astype(BF)
 
-    select(0)
     pl.semaphore_wait(barrier, PLANE - 1 + NZ - 1 + 1)
 
     def hop(stream, way, d, src_z):
@@ -158,9 +157,8 @@
         blocks = sel.at[0, pl.ds(0, ROWS - 2 * CAP)]
         pltpu.make_async_copy(blocks, blocks, sem).wait()
 
-    dispatch(0)
-    for s in range(1, NZ):
-        if s <= 4:
+    for s in OUTWARD:
+        if 1 <= s <= 4:
             arrive(s)
         select(s)
         dispatch(s)
@@ -248,7 +246,7 @@
         zz = (z + s) % NZ
         inner = dot(gath[zz, TOK : 2 * TOK, :], rret[s], 1, 1)
         inner = inner * mats[s, 3 * TOK : 4 * TOK, :].astype(F32)
-        info = meta[zz]
+        info = meta[zz].T[0:TOK]
         quot = jnp.zeros((TOK, 128), F32)
         for k in range(TOP):
             hit = info[:, k : k + 1] == ids
@@ -292,7 +290,7 @@
 
         @pl.when(i > 2)
         def _():
-            gather_home(i - 3, (i == 5) | (i == 7))
+            gather_home(i - 3, i > 5)
 
     go_home(NZ - 1)
 
@@ -314,13 +312,23 @@
     for c in stores:
         c.start()
     quot = jnp.zeros((TOP, 128), F32)
-    for s in range(1, NZ):
+    for s in range(1, NZ - 1):
         leave_inner(s).wait_recv()
         quot += zqx[s]
     total = jnp.zeros((2 * TOK, HALF), F32)
     for s in (1, 2, 3):
         leave(s).wait_recv()
         total += zx[s].astype(F32)
+    for c in hops:
+        c.wait_send()
+    for s in range(NZ):
+        bulk(pd_s.at[s])
+    for s in range(1, NZ - 1):
+        bulk(pr_s.at[s])
+        leave(s).wait_send()
+        leave_inner(s).wait_send()
+    for c in stores:
+        c.wait()
     bulk(pr_r.at[0])
     mx, tg = sums_of(0)
     leave(NZ - 1).wait_recv()
@@ -333,6 +341,8 @@
     ]
     last[0].start()
     quot += inner_of(0)
+    leave_inner(NZ - 1).wait_recv()
+    quot += zqx[NZ - 1]
     finq[...] = quot
     last[1].start()
     mixed_o[:, mine] = fin[0:TOK, :]
@@ -343,16 +353,10 @@
     tgrad_o[:, other] = finr[TOK : 2 * TOK, :]
     gg_o[...] = (quot + finqr[...])[:, 0:TOK]
 
-    for c in hops:
-        c.wait_send()
-    for s in range(NZ):
-        bulk(pd_s.at[s])
-        bulk(pr_s.at[s])
-        if s:
-            leave(s).wait_send()
-            leave_inner(s).wait_send()
-    for c in stores:
-        c.wait()
+    bulk(pr_s.at[0])
+    bulk(pr_s.at[NZ - 1])
+    leave(NZ - 1).wait_send()
+    leave_inner(NZ - 1).wait_send()
 
 
 def place(*refs):
@@ -386,7 +390,7 @@
             pltpu.VMEM((TOP, TOK), jnp.int32),
             pltpu.VMEM((TOP, TOK), F32),
             pltpu.VMEM((NZ, 2 * TOK, HALF), BF),
-            pltpu.VMEM((NZ, TOK, 128), F32),
+            pltpu.VMEM((NZ, 2 * TOP, 128), F32),
             pltpu.VMEM((NZ, 4 * TOK, ROWS), BF),
             pltpu.VMEM((NZ, ROWS, HALF), BF),
             pltpu.VMEM((NZ, ROWS, D), BF),

time: 119 us -> 117 us (0.983)
  Pallas kernels: 118 us -> 116 us
    pallas_call x1, Pallas kernels: 116 us -> 114 us  [body(): pl.pallas_call(kernel, out_shape=shapes, in_specs=[pl.BlockSpec(memory_sp...]
where the time goes in v5:
time: 117 us
  Pallas kernels  116 us (99%)
    pallas_call x1, Pallas kernels, body(): pl.pallas_call(kernel, out_shape=shapes, in_specs=[pl.BlockSpec(memory_sp...  114 us
    pallas_call x1, Pallas kernels, body(): pl.pallas_call(place, out_shape=shapes, in_specs=[vm] * 6, out_specs=[hbm...  2.41 us

profile of v5, /device:TPU:1, one launch (start us, length us, event | category | flops | bytes accessed | tf_op | source)
XLA Modules:
  0.0 116.7 jit_solution(18230329875318733329)
XLA Ops:
  0.6 113.7 %moe.1 = (bf16[64,2048]{1,0:T(8,128)(2,1)S(1)}, bf16[64,2048]{1,0:T(8,128)(2,1)S(1)}, f32[8,64]{1,0:T(8,128)S(1)}, bf16[1,2048,384]{2,1,0:T(8,128)(2,1)S(1)}, bf...) custom-call(bf16[64,2048]{1,0:T(8,128)(2,1)} %tok.1, bf16[64,2048]{1,0:T(8,128)(2,1)} %cot.1, ...), custom_call_target="tpu_custom_call" | custom-call | tf_op jit(solution)/shard_map/moe/pallas_call | solution.py:384
  114.3 2.4 %place.1 = (bf16[64,2048]{1,0:T(8,128)(2,1)}, bf16[64,2048]{1,0:T(8,128)(2,1)}, f32[8,64]{1,0:T(8,128)}, bf16[1,2048,384]{2,1,0:T(8,128)(2,1)}, bf16[1,2048,384]...) custom-call(bf16[64,2048]{1,0:T(8,128)(2,1)S(1)} %get-tuple-element.18.refs_0_, ...), custom_call_target="tpu_custom_call" | custom-call | tf_op jit(solution)/shard_map/place/pallas_call | solution.py:431
